TPU v7x, 512 devices: a whole 4x8x8 slice. The times are simulated.
512 devices in a mesh: seq: 64 (over y_hi, z, core), tp: 8 (over x, y_lo).
Axes of the slice: x: 4, y: 8 (y_hi: 4, y_lo: 2; y = y_hi * 2 + y_lo), z: 8, core: 2. Of those that a mesh axis runs over, the one named last changes fastest.
Arguments:
- frames_in: bfloat16 [1536, 32768], P('tp', 'seq'), may hold values from -30 to 30
- norm_gain: float32 [1536], P('tp'), may hold values from 0.5 to 2
- value_weight: bfloat16 [1536, 1536], P('tp'), may hold values from -0.15625 to 0.15625
- gate_weight: bfloat16 [1536, 1536], P('tp'), may hold values from -0.15625 to 0.15625
- depth_kernel: float32 [1536, 32], P('tp'), may hold values from -6 to 6
- conv_gain: float32 [1536], P('tp'), may hold values from 0.5 to 2
- out_weight: bfloat16 [1536, 1536], P('tp'), may hold values from -0.15625 to 0.15625
- cotangent: bfloat16 [1536, 32768], P('tp', 'seq'), may hold values from -15 to 15
Outputs:
- block_out: bfloat16 [1536, 32768], P('tp', 'seq')
- input_grad: bfloat16 [1536, 32768], P('tp', 'seq')
- grad_norm_gain: float32 [1536], P('tp')
- grad_value: bfloat16 [1536, 1536], P('tp')
- grad_gate: bfloat16 [1536, 1536], P('tp')
- grad_kernel: float32 [1536, 32], P('tp')
- grad_conv_gain: float32 [1536], P('tp')
- grad_out: bfloat16 [1536, 1536], P('tp')
All inputs are finite; a program needn't handle non-finite values.
Results may differ from a plain program's by a relative error of at most 0.027.
Values may be sent and summed in bfloat16 or wider, within the bound.
A program may use at most 64 MiB of HBM per device.

v0:
```python
import jax
import jax.numpy as jnp
from jax import lax
from jax.sharding import PartitionSpec as P

EPS = 1e-05


def with_halo(cells, sides, width):
    for axis, dim in sides:
        count = lax.axis_size(axis)
        ends = count - 1
        head = lax.slice_in_dim(cells, 0, width, axis=dim)
        tail = lax.slice_in_dim(cells, cells.shape[dim] - width, cells.shape[dim], axis=dim)
        cells = jnp.concatenate(
            [
                lax.ppermute(tail, axis, [(i, (i + 1) % count) for i in range(ends)]),
                cells,
                lax.ppermute(head, axis, [((i + 1) % count, i) for i in range(ends)]),
            ],
            axis=dim,
        )
    return cells


def widen(values):
    return lax.optimization_barrier(values).astype(jnp.float32)


def row_sums(values):
    return lax.psum(values, "tp")


def split_norm(values, width):
    mean = row_sums(jnp.sum(values, axis=0, keepdims=True)) / width
    centred = values - mean
    spread = row_sums(jnp.sum(centred * centred, axis=0, keepdims=True)) / width
    inverse = lax.rsqrt(spread + EPS)
    return (centred * inverse, inverse)


def split_norm_back(d_hat, hat, inverse, width):
    first, second = row_sums(
        (jnp.sum(d_hat, axis=0, keepdims=True), jnp.sum(d_hat * hat, axis=0, keepdims=True))
    )
    return (d_hat - first / width - hat * (second / width)) * inverse


def spread_channels(values):
    return lax.all_gather(values, "tp", axis=0, tiled=True)


def frame_rims(values, reach):
    return with_halo(values, (("seq", 1),), reach)


def reduce_inputs(term):
    rounded = widen(term.astype(jnp.bfloat16))
    return lax.psum_scatter(
        rounded.astype(jnp.bfloat16), "tp", scatter_dimension=0, tiled=True
    ).astype(jnp.float32)


def contract_rows(left, right):
    return lax.dot_general(
        left, right, (((0,), (0,)), ((), ())), preferred_element_type=jnp.float32
    )


def contract_cols(left, right):
    return lax.dot_general(
        left, right, (((1,), (1,)), ((), ())), preferred_element_type=jnp.float32
    )


def local(
    frames_in, norm_gain, value_weight, gate_weight, depth_kernel, conv_gain, out_weight, cotangent
):
    chans, row_count = frames_in.shape
    parts = lax.axis_size("tp")
    width = chans * parts
    taps = depth_kernel.shape[1]
    reach = taps // 2
    scale = float(row_count * lax.axis_size("seq")) ** (-0.5)
    inputs = frames_in.astype(jnp.float32)
    hat_in, inverse_in = split_norm(inputs, width)
    normed = (hat_in * norm_gain[:, None]).astype(jnp.bfloat16)
    normed_all = spread_channels(normed)
    value = jnp.dot(value_weight, normed_all, preferred_element_type=jnp.float32)
    gate = jnp.dot(gate_weight, normed_all, preferred_element_type=jnp.float32)
    gate_sig = jax.nn.sigmoid(gate)
    glu = (value * gate_sig).astype(jnp.bfloat16)
    glu_wide = widen(frame_rims(glu, reach))
    conv = jnp.zeros((chans, row_count), jnp.float32)
    for tap in range(taps):
        conv = conv + depth_kernel[:, tap : tap + 1] * glu_wide[:, tap : tap + row_count]
    hat_conv, inverse_conv = split_norm(conv, width)
    scaled = hat_conv * conv_gain[:, None]
    swish_sig = jax.nn.sigmoid(scaled)
    act = (scaled * swish_sig).astype(jnp.bfloat16)
    act_all = spread_channels(act)
    block_out = (inputs + jnp.dot(out_weight, act_all, preferred_element_type=jnp.float32)).astype(
        jnp.bfloat16
    )
    grad_out = contract_cols(cotangent, act_all) * scale
    d_act = reduce_inputs(contract_rows(out_weight, cotangent))
    d_scaled = d_act * (swish_sig + scaled * swish_sig * (1.0 - swish_sig))
    grad_conv_gain = jnp.sum(d_scaled * hat_conv, axis=1) * scale
    d_conv = split_norm_back(d_scaled * conv_gain[:, None], hat_conv, inverse_conv, width).astype(
        jnp.bfloat16
    )
    d_conv_f = widen(d_conv)
    d_conv_wide = widen(frame_rims(d_conv, reach))
    d_glu = jnp.zeros((chans, row_count), jnp.float32)
    kernel_cols = []
    for tap in range(taps):
        start = 2 * reach - tap
        d_glu = d_glu + depth_kernel[:, tap : tap + 1] * d_conv_wide[:, start : start + row_count]
        kernel_cols.append(jnp.sum(glu_wide[:, tap : tap + row_count] * d_conv_f, axis=1))
    grad_kernel = jnp.stack(kernel_cols, axis=1) * scale
    d_value = (d_glu * gate_sig).astype(jnp.bfloat16)
    d_gate = (d_glu * value * gate_sig * (1.0 - gate_sig)).astype(jnp.bfloat16)
    grad_value = contract_cols(d_value, normed_all) * scale
    grad_gate = contract_cols(d_gate, normed_all) * scale
    d_normed = reduce_inputs(
        contract_rows(value_weight, d_value) + contract_rows(gate_weight, d_gate)
    )
    grad_norm_gain = jnp.sum(d_normed * hat_in, axis=1) * scale
    input_grad = (
        cotangent.astype(jnp.float32)
        + split_norm_back(d_normed * norm_gain[:, None], hat_in, inverse_in, width)
    ).astype(jnp.bfloat16)
    grad_out, grad_kernel, grad_conv_gain, grad_value, grad_gate, grad_norm_gain = lax.psum(
        (grad_out, grad_kernel, grad_conv_gain, grad_value, grad_gate, grad_norm_gain), "seq"
    )
    return (
        block_out,
        input_grad,
        grad_norm_gain,
        grad_value.astype(jnp.bfloat16),
        grad_gate.astype(jnp.bfloat16),
        grad_kernel,
        grad_conv_gain,
        grad_out.astype(jnp.bfloat16),
    )


def solution(mesh):
    return jax.shard_map(
        local,
        mesh=mesh,
        in_specs=(
            P("tp", "seq"),
            P("tp"),
            P("tp", None),
            P("tp", None),
            P("tp", None),
            P("tp"),
            P("tp", None),
            P("tp", "seq"),
        ),
        out_specs=(
            P("tp", "seq"),
            P("tp", "seq"),
            P("tp"),
            P("tp", None),
            P("tp", None),
            P("tp", None),
            P("tp"),
            P("tp", None),
        ),
        check_vma=False,
    )
```

profile of v0, /device:TPU:2, one launch (start us, length us, event | category | flops | bytes accessed | tf_op | source)
XLA Modules:
  0.0 620.3 jit_solution(990302388884489150)
XLA Ops:
  7.2 1.0 convert_reduce_fusion
  8.3 19.2 %psum.98 = f32[1,512]{1,0:T(1,128)S(1)} all-reduce(f32[1,512]{1,0:T(1,128)S(1)} %bitcast.194), channel_id=1, replica_groups=mesh['seq'=64,'tp'=8] {'tp'}, use_global_device_ids=true, to_apply=%region_1.0 | all-reduce | flops 512 | bytes 4096 | tf_op jit(solution)/shard_map/psum | solution.py:31
  27.5 1.0 fusion.21
  28.5 18.0 %psum.99 = f32[1,512]{1,0:T(1,128)S(1)} all-reduce(f32[1,512]{1,0:T(1,128)S(1)} %bitcast.195), channel_id=1, replica_groups=mesh['seq'=64,'tp'=8] {'tp'}, use_global_device_ids=true, to_apply=%region_3.0 | all-reduce | flops 512 | bytes 4096 | tf_op jit(solution)/shard_map/psum | solution.py:31
  46.5 1.7 fusion.16
  48.3 2.9 convolution_convert_fusion
  51.4 44.4 %all-gather.3.cloned.1.call-done = bf16[1536,512]{1,0:T(8,128)(2,1)} async-done(((bf16[192,512]{1,0:T(8,128)(2,1)}), bf16[1536,512]{1,0:T(8,128)(2,1)}) %all-gather.3.cloned.1.call-update) | async-done | bytes 1572880 | tf_op jit(solution)/shard_map/all_gather | solution.py:50
  95.8 2.1 fusion.6
  97.9 1.2 multiply_convert_fusion.3
  99.1 0.1 fusion.91
  99.2 1.3 collective-permute-start
  100.5 1.3 collective-permute-start.1
  101.9 3.6 collective-permute-done.1
  105.5 0.1 pad_maximum_fusion
  105.7 4.6 fusion.89
  110.4 18.3 %psum.100 = f32[1,512]{1,0:T(1,128)S(1)} all-reduce(f32[1,512]{1,0:T(1,128)S(1)} %bitcast.199), channel_id=1, replica_groups=mesh['seq'=64,'tp'=8] {'tp'}, use_global_device_ids=true, to_apply=%region_5.0 | all-reduce | flops 512 | bytes 4096 | tf_op jit(solution)/shard_map/psum | solution.py:31
  128.8 0.1 multiply_reduce_fusion.2
  128.8 16.7 %psum.101 = f32[1,512]{1,0:T(1,128)S(1)} all-reduce(f32[1,512]{1,0:T(1,128)S(1)} %bitcast.196), channel_id=1, replica_groups=mesh['seq'=64,'tp'=8] {'tp'}, use_global_device_ids=true, to_apply=%region_7.0 | all-reduce | flops 512 | bytes 4096 | tf_op jit(solution)/shard_map/psum | solution.py:31
  145.5 1.7 reduce-scatter.3.cloned.1.call-done
  147.3 2.6 multiply_reduce_fusion
  149.8 18.2 %all-reduce.2 = (f32[1,512]{1,0:T(1,128)S(1)}, f32[1,512]{1,0:T(1,128)S(1)}) all-reduce(f32[1,512]{1,0:T(1,128)S(1)} %bitcast.190, f32[1,512]{1,0:T(1,128)S(1)} %bitcast.191), channel_id=1, replica_groups=mesh['seq'=64,'tp'=8] {'tp'}, use_global_device_ids=true, to_apply=%region_12.0 | all-reduce | flops 1024 | bytes 8192 | tf_op jit(solution)/shard_map/psum | solution.py:31
  168.0 1.9 multiply_convert_fusion.2
  170.0 0.1 fusion.90
  170.1 1.3 collective-permute-start.2
  171.4 1.5 collective-permute-start.3
  172.9 3.5 collective-permute-done.3
  176.4 0.1 pad_maximum_fusion.1
  176.6 5.8 multiply_convert_fusion
  182.5 0.7 fusion.94
  183.2 0.4 copy-done.12
  183.6 1.8 fusion.1
  185.5 2.1 fusion.54
  187.6 2.8 fusion.55
  190.3 0.1 stack.131
  190.5 0.6 broadcast_multiply_fusion.7
  191.0 0.6 broadcast_multiply_fusion
  191.6 0.7 convolution_multiply_fusion.1
  192.3 2.7 convolution_multiply_fusion.2
  195.0 22.7 %all-gather.5.cloned.1.call-done = bf16[1536,512]{1,0:T(8,128)(2,1)} async-done(((bf16[192,512]{1,0:T(8,128)(2,1)}), bf16[1536,512]{1,0:T(8,128)(2,1)}) %all-gather.5.cloned.1.call-update) | async-done | bytes 1572880 | tf_op jit(solution)/shard_map/all_gather | solution.py:50
  217.7 3.2 fusion.2
  221.0 1.2 fusion.8
  222.2 46.4 %reduce-scatter.5.cloned.1.call-done = bf16[192,512]{1,0:T(8,128)(2,1)} async-done(((bf16[1536,512]{1,0:T(8,128)(2,1)}), bf16[192,512]{1,0:T(8,128)(2,1)}) %reduce-scatter.5.cloned.1.call-update) | async-done | bytes 196624 | tf_op jit(solution)/shard_map/reduce_scatter | solution.py:59
  268.6 1.1 fusion.23
  269.7 0.6 broadcast_multiply_fusion.8
  270.3 18.3 %all-reduce.1 = (f32[1,512]{1,0:T(1,128)S(1)}, f32[1,512]{1,0:T(1,128)S(1)}) all-reduce(f32[1,512]{1,0:T(1,128)S(1)} %bitcast.192, f32[1,512]{1,0:T(1,128)S(1)} %bitcast.193), channel_id=1, replica_groups=mesh['seq'=64,'tp'=8] {'tp'}, use_global_device_ids=true, to_apply=%region_17.0 | all-reduce | flops 1024 | bytes 8192 | tf_op jit(solution)/shard_map/psum | solution.py:31
  288.7 0.6 broadcast_multiply_fusion.2
  289.3 323.0 %all-reduce.4 = (f32[192]{0:T(256)}, bf16[192,1536]{1,0:T(8,128)(2,1)}, bf16[192,1536]{1,0:T(8,128)(2,1)}, f32[192,32]{0,1:T(8,128)}, f32[192]{0:T(256)}, /*index=5*/bf16[192,1536]{1,0:T(8,128)(2,1)}) all-reduce(f32[192]{0:T(256)} %broadcast_multiply_fusion.8, ...), channel_id=1, replica_groups=mesh['seq'=64,'tp'=8] {'seq'}, use_global_device_ids=true, to_apply=%region_19.0 | all-reduce | flops 891264 | bytes 5360640 | tf_op jit(solution)/shard_map/psum | solution.py:133
  612.3 1.5 fusion.20
  (70 shorter events, 0.6 us)
Async XLA Ops:
  7.2 90.7 %copy-start = (bf16[192,1536]{1,0:T(8,128)(2,1)S(1)}, bf16[192,1536]{1,0:T(8,128)(2,1)}, u32[]{:S(2)}) copy-start(bf16[192,1536]{1,0:T(8,128)(2,1)} %param.10) | copy-start | bytes 1769476
  7.2 88.6 %all-gather.3.cloned.1.call-start = ((), (), s32[]{:S(2)}) async-start(), calls=%async_computation.2 | async-start | bytes 1769472 | tf_op jit(solution)/shard_map/all_gather | solution.py:50
  48.3 3.1 copy-start.13
  48.3 47.5 %copy-start.11 = (bf16[192,1536]{1,0:T(8,128)(2,1)S(1)}, bf16[192,1536]{1,0:T(8,128)(2,1)}, u32[]{:S(2)}) copy-start(bf16[192,1536]{1,0:T(8,128)(2,1)} %param.11) | copy-start | bytes 1769476
  48.3 99.0 %reduce-scatter.3.cloned.1.call-start = ((), (), s32[]{:S(2)}) async-start(), calls=%async_computation.4 | async-start | bytes 1769472 | tf_op jit(solution)/shard_map/reduce_scatter | solution.py:59
  51.3 166.4 %all-gather.5.cloned.1.call-start = ((), (), s32[]{:S(2)}) async-start(), calls=%async_computation.3 | async-start | bytes 1769472 | tf_op jit(solution)/shard_map/all_gather | solution.py:50
  95.8 2.1 copy-start.1
  97.9 1.2 copy-start.5
  99.2 2.7 collective-permute-start
  100.5 5.0 collective-permute-start.1
  101.8 8.5 %copy-start.15 = (f32[192,1]{0,1:T(1,128)}, f32[192,1]{0,1:T(1,128)S(1)}, u32[]{:S(2)}) copy-start(f32[192,1]{0,1:T(1,128)S(1)} %get-tuple-element.91) | copy-start | bytes 2308
  101.8 8.5 %copy-start.16 = (f32[192,1]{0,1:T(1,128)}, f32[192,1]{0,1:T(1,128)S(1)}, u32[]{:S(2)}) copy-start(f32[192,1]{0,1:T(1,128)S(1)} %get-tuple-element.92) | copy-start | bytes 2308
  101.8 8.5 %copy-start.17 = (f32[192,1]{0,1:T(1,128)}, f32[192,1]{0,1:T(1,128)S(1)}, u32[]{:S(2)}) copy-start(f32[192,1]{0,1:T(1,128)S(1)} %get-tuple-element.93) | copy-start | bytes 2308
  101.8 8.5 %copy-start.18 = (f32[192,1]{0,1:T(1,128)}, f32[192,1]{0,1:T(1,128)S(1)}, u32[]{:S(2)}) copy-start(f32[192,1]{0,1:T(1,128)S(1)} %get-tuple-element.94) | copy-start | bytes 2308
  101.9 8.5 %copy-start.19 = (f32[192,1]{0,1:T(1,128)}, f32[192,1]{0,1:T(1,128)S(1)}, u32[]{:S(2)}) copy-start(f32[192,1]{0,1:T(1,128)S(1)} %get-tuple-element.95) | copy-start | bytes 2308
  101.9 8.5 %copy-start.20 = (f32[192,1]{0,1:T(1,128)}, f32[192,1]{0,1:T(1,128)S(1)}, u32[]{:S(2)}) copy-start(f32[192,1]{0,1:T(1,128)S(1)} %get-tuple-element.96) | copy-start | bytes 2308
  101.9 8.5 %copy-start.21 = (f32[192,1]{0,1:T(1,128)}, f32[192,1]{0,1:T(1,128)S(1)}, u32[]{:S(2)}) copy-start(f32[192,1]{0,1:T(1,128)S(1)} %get-tuple-element.97) | copy-start | bytes 2308
  101.9 8.5 %copy-start.22 = (f32[192,1]{0,1:T(1,128)}, f32[192,1]{0,1:T(1,128)S(1)}, u32[]{:S(2)}) copy-start(f32[192,1]{0,1:T(1,128)S(1)} %get-tuple-element.98) | copy-start | bytes 2308
  105.7 41.6 %copy-start.24 = (f32[192]{0:T(256)S(1)}, f32[192]{0:T(256)}, u32[]{:S(2)}) copy-start(f32[192]{0:T(256)} %param.13) | copy-start | bytes 2308
  170.0 98.6 %reduce-scatter.5.cloned.1.call-start = ((), (), s32[]{:S(2)}) async-start(), calls=%async_computation.5 | async-start | bytes 1769472 | tf_op jit(solution)/shard_map/reduce_scatter | solution.py:59
  170.1 2.8 collective-permute-start.2
  171.4 5.0 collective-permute-start.3
  176.6 5.8 copy-start.6
  182.5 0.7 copy-start.9
  182.5 1.1 copy-start.12
  187.6 2.9 copy-start.23
  192.3 25.4 %copy-start.8 = (bf16[192,512]{1,0:T(8,128)(2,1)S(1)}, bf16[192,512]{1,0:T(8,128)(2,1)}, u32[]{:S(2)}) copy-start(bf16[192,512]{1,0:T(8,128)(2,1)} %param.15) | copy-start | bytes 589828
  195.0 26.0 %copy-start.2 = (bf16[192,512]{1,0:T(8,128)(2,1)S(1)}, bf16[192,512]{1,0:T(8,128)(2,1)}, u32[]{:S(2)}) copy-start(bf16[192,512]{1,0:T(8,128)(2,1)} %param.8) | copy-start | bytes 589828
  217.7 3.3 copy-start.3
  217.7 3.3 copy-start.7
  221.0 47.6 %copy-start.14 = (f32[192]{0:T(256)S(1)}, f32[192]{0:T(256)}, u32[]{:S(2)}) copy-start(f32[192]{0:T(256)} %param.9) | copy-start | bytes 2308
  221.0 68.2 %copy-start.4 = (f32[192,1536]{1,0:T(8,128)S(1)}, f32[192,1536]{1,0:T(8,128)}, u32[]{:S(2)}) copy-start(f32[192,1536]{1,0:T(8,128)} %convolution_multiply_fusion.2) | copy-start | bytes 3538948
  289.3 323.0 %copy-start.10 = (bf16[192,512]{1,0:T(8,128)(2,1)S(1)}, bf16[192,512]{1,0:T(8,128)(2,1)}, u32[]{:S(2)}) copy-start(bf16[192,512]{1,0:T(8,128)(2,1)} %reduce-scatter.5.cloned.1.call-done) | copy-start | bytes 589828
Sparse Core Ops, SparseCore 0:
  48.4 47.3 all-gather.2
  98.6 48.5 reduce-scatter.2
  170.1 47.5 all-gather.4
  220.4 48.1 reduce-scatter.4
where the time goes:
time: 621 us; the launch traced here: 620 us
  blocking collectives  432 us (70%)
  waiting for transfers between devices  122 us (20%)
  other arithmetic  29 us (5%)
  matrix products  16.4 us (3%)
  between operations  14.2 us (2%)
    psum x1, blocking collectives, local(): lax.psum((grad_out, grad_kernel, grad_conv_gain, grad_value, grad_gate, g...  323 us
    psum x6, blocking collectives, row_sums(): return lax.psum(values, 'tp')  109 us
    all_gather x2, waiting for transfers between devices, spread_channels(): return lax.all_gather(values, 'tp', axis=0, tiled=True)  67.1 us
    reduce_scatter x2, waiting for transfers between devices, reduce_inputs(): lax.psum_scatter(rounded.astype(jnp.bfloat16), 'tp', scatter_dimension=0,...  48.2 us
  transfers between devices with their start and end apart: 8, of which 6 were waited for; matrix products, arithmetic and copies ran while one was open for 5% of the time, Pallas kernels for 0%

commit v1 on v0

--- a/solution.py
+++ b/solution.py
@@ -1,9 +1,19 @@
+import functools
 import jax
 import jax.numpy as jnp
 from jax import lax
 from jax.sharding import PartitionSpec as P
 
 EPS = 1e-05
+
+
+def review_thing(panel, net_axis):
+    y_new = jnp.stack([panel] * lax.psum(1, net_axis))
+    seen_now = lax.all_to_all(y_new, net_axis, 0, 0)
+    return jnp.concatenate(seen_now, 0)
+
+
+search_the_rates = functools.partial(review_thing, net_axis="tp")
 
 
 def with_halo(cells, sides, width):
@@ -47,7 +57,7 @@
 
 
 def spread_channels(values):
-    return lax.all_gather(values, "tp", axis=0, tiled=True)
+    return search_the_rates(values)
 
 
 def frame_rims(values, reach):

time: 621 us -> 564 us (0.908)
  the two profiles are of different devices: /device:TPU:2 before, /device:TPU:32 now
where the time goes in v1:
time: 564 us; the launch traced here: 563 us
  blocking collectives  427 us (76%)
  waiting for transfers between devices  44.6 us (8%)
  starting transfers between devices  28 us (5%)
  other arithmetic  27.5 us (5%)
  matrix products  15.2 us (3%)
  between operations  14.8 us (3%)
    psum x1, blocking collectives, local(): lax.psum((grad_out, grad_kernel, grad_conv_gain, grad_value, grad_gate, g...  322 us
    psum x6, blocking collectives, row_sums(): return lax.psum(values, 'tp')  106 us
    reduce_scatter x2, waiting for transfers between devices, reduce_inputs(): lax.psum_scatter(rounded.astype(jnp.bfloat16), 'tp', scatter_dimension=0,...  30.8 us
    ppermute x2, starting transfers between devices, with_halo(): lax.ppermute(head, axis, [((i + 1) % count, i) for i in range(ends)])  15.7 us
    all_to_all x2, waiting for transfers between devices, review_thing(): seen_now = lax.all_to_all(y_new, net_axis, 0, 0)  12.2 us
  transfers between devices with their start and end apart: 8, of which 4 were waited for; matrix products, arithmetic and copies ran while one was open for 6% of the time, Pallas kernels for 0%

profile of v1, /device:TPU:32, one launch (start us, length us, event | category | flops | bytes accessed | tf_op | source)
XLA Modules:
  0.0 563.0 jit_solution(2144543043569298078)
XLA Ops:
  7.2 1.0 convert_reduce_fusion
  8.2 18.9 %psum.98 = f32[1,512]{1,0:T(1,128)S(1)} all-reduce(f32[1,512]{1,0:T(1,128)S(1)} %bitcast.200), channel_id=1, replica_groups=mesh['seq'=64,'tp'=8] {'tp'}, use_global_device_ids=true, to_apply=%region_1.0 | all-reduce | flops 512 | bytes 4096 | tf_op jit(solution)/shard_map/psum | solution.py:41
  27.1 1.0 fusion.21
  28.1 16.1 %psum.99 = f32[1,512]{1,0:T(1,128)S(1)} all-reduce(f32[1,512]{1,0:T(1,128)S(1)} %bitcast.201), channel_id=1, replica_groups=mesh['seq'=64,'tp'=8] {'tp'}, use_global_device_ids=true, to_apply=%region_3.0 | all-reduce | flops 512 | bytes 4096 | tf_op jit(solution)/shard_map/psum | solution.py:41
  44.2 1.0 fusion.16
  45.2 1.3 stack.121
  46.5 3.7 all-to-all-start
  50.3 1.8 convolution_convert_fusion
  52.1 0.7 copy-done.13
  52.8 0.7 fusion.92
  53.5 12.2 %all-to-all-done = bf16[8,192,512]{2,1,0:T(8,128)(2,1)S(1)} async-done(((bf16[8,192,512]{2,1,0:T(8,128)(2,1)}), bf16[8,192,512]{2,1,0:T(8,128)(2,1)S(1)}, u32[]{:S(2)}, u32[]{:S(2)}) %all-to-all-start) | async-done | bytes 1572896 | tf_op jit(solution)/shard_map/all_to_all | solution.py:12
  65.7 0.5 fusion.6
  66.2 1.2 multiply_convert_fusion.3
  67.7 1.9 collective-permute-start
  69.6 7.9 %collective-permute-start.1 = (bf16[192,16]{1,0:T(8,128)(2,1)S(1)}, bf16[192,16]{1,0:T(8,128)(2,1)S(1)}, u32[]{:S(2)}, u32[]{:S(2)}) collective-permute-start(bf16[192,16]{1,0:T(8,128)(2,1)S(1)} %get-tuple-element.66), channel_id=1, source_target_pairs={{8,0},{16,8},{24,16},{32,24},{40,32},{48,40},{56,48},{64,56},{72,6... | collective-permute-start | bytes 18440 | tf_op jit(solution)/shard_map/ppermute | solution.py:29
  77.6 0.4 collective-permute-done
  78.0 1.2 collective-permute-done.1
  79.7 4.6 fusion.89
  84.4 18.4 %psum.100 = f32[1,512]{1,0:T(1,128)S(1)} all-reduce(f32[1,512]{1,0:T(1,128)S(1)} %bitcast.205), channel_id=1, replica_groups=mesh['seq'=64,'tp'=8] {'tp'}, use_global_device_ids=true, to_apply=%region_5.0 | all-reduce | flops 512 | bytes 4096 | tf_op jit(solution)/shard_map/psum | solution.py:41
  102.9 16.0 %psum.101 = f32[1,512]{1,0:T(1,128)S(1)} all-reduce(f32[1,512]{1,0:T(1,128)S(1)} %bitcast.202), channel_id=1, replica_groups=mesh['seq'=64,'tp'=8] {'tp'}, use_global_device_ids=true, to_apply=%region_7.0 | all-reduce | flops 512 | bytes 4096 | tf_op jit(solution)/shard_map/psum | solution.py:41
  119.0 2.6 multiply_reduce_fusion
  121.6 18.1 %all-reduce.2 = (f32[1,512]{1,0:T(1,128)S(1)}, f32[1,512]{1,0:T(1,128)S(1)}) all-reduce(f32[1,512]{1,0:T(1,128)S(1)} %bitcast.196, f32[1,512]{1,0:T(1,128)S(1)} %bitcast.197), channel_id=1, replica_groups=mesh['seq'=64,'tp'=8] {'tp'}, use_global_device_ids=true, to_apply=%region_12.0 | all-reduce | flops 1024 | bytes 8192 | tf_op jit(solution)/shard_map/psum | solution.py:41
  139.6 1.2 multiply_convert_fusion.2
  141.0 1.9 collective-permute-start.2
  142.9 7.9 %collective-permute-start.3 = (bf16[192,16]{1,0:T(8,128)(2,1)S(1)}, bf16[192,16]{1,0:T(8,128)(2,1)S(1)}, u32[]{:S(2)}, u32[]{:S(2)}) collective-permute-start(bf16[192,16]{1,0:T(8,128)(2,1)S(1)} %get-tuple-element.64), channel_id=1, source_target_pairs={{8,0},{16,8},{24,16},{32,24},{40,32},{48,40},{56,48},{64,56},{72,6... | collective-permute-start | bytes 18440 | tf_op jit(solution)/shard_map/ppermute | solution.py:29
  150.8 1.3 stack.122
  152.0 4.4 all-to-all-start.1
  156.5 0.2 reduce-scatter.5.cloned.1.call-start
  156.9 5.6 multiply_convert_fusion
  162.6 0.7 copy-done.9
  163.3 0.7 fusion.94
  164.0 0.4 copy-done.12
  164.4 1.8 fusion.1
  166.2 2.1 fusion.54
  168.3 2.8 fusion.55
  171.2 0.6 broadcast_multiply_fusion.7
  171.7 0.6 broadcast_multiply_fusion
  172.3 0.7 convolution_multiply_fusion.1
  173.0 2.7 convolution_multiply_fusion.2
  175.7 3.2 fusion.2
  178.9 2.7 fusion.8
  181.6 30.8 %reduce-scatter.5.cloned.1.call-done = bf16[192,512]{1,0:T(8,128)(2,1)} async-done(((bf16[1536,512]{1,0:T(8,128)(2,1)}), bf16[192,512]{1,0:T(8,128)(2,1)}) %reduce-scatter.5.cloned.1.call-update) | async-done | bytes 196624 | tf_op jit(solution)/shard_map/reduce_scatter | solution.py:69
  212.4 1.1 fusion.23
  213.5 0.6 broadcast_multiply_fusion.8
  214.1 18.0 %all-reduce.1 = (f32[1,512]{1,0:T(1,128)S(1)}, f32[1,512]{1,0:T(1,128)S(1)}) all-reduce(f32[1,512]{1,0:T(1,128)S(1)} %bitcast.198, f32[1,512]{1,0:T(1,128)S(1)} %bitcast.199), channel_id=1, replica_groups=mesh['seq'=64,'tp'=8] {'tp'}, use_global_device_ids=true, to_apply=%region_17.0 | all-reduce | flops 1024 | bytes 8192 | tf_op jit(solution)/shard_map/psum | solution.py:41
  232.1 0.6 broadcast_multiply_fusion.2
  232.7 321.9 %all-reduce.4 = (f32[192]{0:T(256)}, bf16[192,1536]{1,0:T(8,128)(2,1)}, bf16[192,1536]{1,0:T(8,128)(2,1)}, f32[192,32]{0,1:T(8,128)}, f32[192]{0:T(256)}, /*index=5*/bf16[192,1536]{1,0:T(8,128)(2,1)}) all-reduce(f32[192]{0:T(256)} %broadcast_multiply_fusion.8, ...), channel_id=1, replica_groups=mesh['seq'=64,'tp'=8] {'seq'}, use_global_device_ids=true, to_apply=%region_19.0 | all-reduce | flops 891264 | bytes 5360640 | tf_op jit(solution)/shard_map/psum | solution.py:143
  554.6 1.5 fusion.20
  (114 shorter events, 1.1 us)
Async XLA Ops:
  7.2 59.0 %copy-start = (bf16[192,1536]{1,0:T(8,128)(2,1)S(1)}, bf16[192,1536]{1,0:T(8,128)(2,1)}, u32[]{:S(2)}) copy-start(bf16[192,1536]{1,0:T(8,128)(2,1)} %param.10) | copy-start | bytes 1769476
  46.5 3.8 copy-start.5
  46.5 3.8 copy-start.7
  46.5 19.1 %all-to-all-start = ((bf16[8,192,512]{2,1,0:T(8,128)(2,1)}), bf16[8,192,512]{2,1,0:T(8,128)(2,1)S(1)}, u32[]{:S(2)}, u32[]{:S(2)}) async-start(bf16[8,192,512]{2,1,0:T(8,128)(2,1)} %stack.121), calls=%async_computation | async-start | bytes 3145728 | tf_op jit(solution)/shard_map/all_to_all | solution.py:12
  50.2 15.4 %copy-start.11 = (bf16[192,1536]{1,0:T(8,128)(2,1)S(1)}, bf16[192,1536]{1,0:T(8,128)(2,1)}, u32[]{:S(2)}) copy-start(bf16[192,1536]{1,0:T(8,128)(2,1)} %param.11) | copy-start | bytes 1769476
  50.3 68.7 %reduce-scatter.3.cloned.1.call-start = ((), (), s32[]{:S(2)}) async-start(), calls=%async_computation.4 | async-start | bytes 1769472 | tf_op jit(solution)/shard_map/reduce_scatter | solution.py:69
  67.4 12.0 %copy-start.15 = (f32[192,1]{0,1:T(1,128)S(1)}, f32[192,1]{0,1:T(1,128)}, u32[]{:S(2)}) copy-start(f32[192,1]{0,1:T(1,128)} %get-tuple-element.69) | copy-start | bytes 2308
  67.4 12.0 %copy-start.16 = (f32[192,1]{0,1:T(1,128)S(1)}, f32[192,1]{0,1:T(1,128)}, u32[]{:S(2)}) copy-start(f32[192,1]{0,1:T(1,128)} %get-tuple-element.70) | copy-start | bytes 2308
  67.4 12.0 %copy-start.17 = (f32[192,1]{0,1:T(1,128)S(1)}, f32[192,1]{0,1:T(1,128)}, u32[]{:S(2)}) copy-start(f32[192,1]{0,1:T(1,128)} %get-tuple-element.71) | copy-start | bytes 2308
  67.4 12.1 %copy-start.18 = (f32[192,1]{0,1:T(1,128)S(1)}, f32[192,1]{0,1:T(1,128)}, u32[]{:S(2)}) copy-start(f32[192,1]{0,1:T(1,128)} %get-tuple-element.72) | copy-start | bytes 2308
  67.5 12.1 %copy-start.19 = (f32[192,1]{0,1:T(1,128)S(1)}, f32[192,1]{0,1:T(1,128)}, u32[]{:S(2)}) copy-start(f32[192,1]{0,1:T(1,128)} %get-tuple-element.73) | copy-start | bytes 2308
  67.5 12.1 %copy-start.20 = (f32[192,1]{0,1:T(1,128)S(1)}, f32[192,1]{0,1:T(1,128)}, u32[]{:S(2)}) copy-start(f32[192,1]{0,1:T(1,128)} %get-tuple-element.74) | copy-start | bytes 2308
  67.5 12.1 %copy-start.21 = (f32[192,1]{0,1:T(1,128)S(1)}, f32[192,1]{0,1:T(1,128)}, u32[]{:S(2)}) copy-start(f32[192,1]{0,1:T(1,128)} %get-tuple-element.75) | copy-start | bytes 2308
  67.5 12.1 %copy-start.22 = (f32[192,1]{0,1:T(1,128)S(1)}, f32[192,1]{0,1:T(1,128)}, u32[]{:S(2)}) copy-start(f32[192,1]{0,1:T(1,128)} %get-tuple-element.76) | copy-start | bytes 2308
  67.5 12.1 %copy-start.23 = (f32[192,1]{0,1:T(1,128)S(1)}, f32[192,1]{0,1:T(1,128)}, u32[]{:S(2)}) copy-start(f32[192,1]{0,1:T(1,128)} %get-tuple-element.77) | copy-start | bytes 2308
  67.5 12.1 %copy-start.24 = (f32[192,1]{0,1:T(1,128)S(1)}, f32[192,1]{0,1:T(1,128)}, u32[]{:S(2)}) copy-start(f32[192,1]{0,1:T(1,128)} %get-tuple-element.78) | copy-start | bytes 2308
  67.5 12.1 %copy-start.25 = (f32[192,1]{0,1:T(1,128)S(1)}, f32[192,1]{0,1:T(1,128)}, u32[]{:S(2)}) copy-start(f32[192,1]{0,1:T(1,128)} %get-tuple-element.79) | copy-start | bytes 2308
  67.5 12.1 %copy-start.26 = (f32[192,1]{0,1:T(1,128)S(1)}, f32[192,1]{0,1:T(1,128)}, u32[]{:S(2)}) copy-start(f32[192,1]{0,1:T(1,128)} %get-tuple-element.80) | copy-start | bytes 2308
  67.5 12.1 %copy-start.27 = (f32[192,1]{0,1:T(1,128)S(1)}, f32[192,1]{0,1:T(1,128)}, u32[]{:S(2)}) copy-start(f32[192,1]{0,1:T(1,128)} %get-tuple-element.81) | copy-start | bytes 2308
  67.5 12.1 %copy-start.28 = (f32[192,1]{0,1:T(1,128)S(1)}, f32[192,1]{0,1:T(1,128)}, u32[]{:S(2)}) copy-start(f32[192,1]{0,1:T(1,128)} %get-tuple-element.82) | copy-start | bytes 2308
  67.6 12.1 %copy-start.29 = (f32[192,1]{0,1:T(1,128)S(1)}, f32[192,1]{0,1:T(1,128)}, u32[]{:S(2)}) copy-start(f32[192,1]{0,1:T(1,128)} %get-tuple-element.83) | copy-start | bytes 2308
  67.6 12.1 %copy-start.30 = (f32[192,1]{0,1:T(1,128)S(1)}, f32[192,1]{0,1:T(1,128)}, u32[]{:S(2)}) copy-start(f32[192,1]{0,1:T(1,128)} %get-tuple-element.84) | copy-start | bytes 2308
  67.6 12.1 %copy-start.31 = (f32[192,1]{0,1:T(1,128)S(1)}, f32[192,1]{0,1:T(1,128)}, u32[]{:S(2)}) copy-start(f32[192,1]{0,1:T(1,128)} %get-tuple-element.85) | copy-start | bytes 2308
  67.7 10.4 %collective-permute-start = (bf16[192,16]{1,0:T(8,128)(2,1)S(1)}, bf16[192,16]{1,0:T(8,128)(2,1)S(1)}, u32[]{:S(2)}, u32[]{:S(2)}) collective-permute-start(bf16[192,16]{1,0:T(8,128)(2,1)S(1)} %get-tuple-element.65), channel_id=1, source_target_pairs={{0,8},{8,16},{16,24},{24,32},{32,40},{40,48},{48,56},{56,64},{64,7... | collective-permute-start | bytes 18440 | tf_op jit(solution)/shard_map/ppermute | solution.py:27
  69.6 9.7 %collective-permute-start.1 = (bf16[192,16]{1,0:T(8,128)(2,1)S(1)}, bf16[192,16]{1,0:T(8,128)(2,1)S(1)}, u32[]{:S(2)}, u32[]{:S(2)}) collective-permute-start(bf16[192,16]{1,0:T(8,128)(2,1)S(1)} %get-tuple-element.66), channel_id=1, source_target_pairs={{8,0},{16,8},{24,16},{32,24},{40,32},{48,40},{56,48},{64,56},{72,6... | collective-permute-start | bytes 18440 | tf_op jit(solution)/shard_map/ppermute | solution.py:29
  77.5 6.8 %copy-start.32 = (f32[192,1]{0,1:T(1,128)}, f32[192,1]{0,1:T(1,128)S(1)}, u32[]{:S(2)}) copy-start(f32[192,1]{0,1:T(1,128)S(1)} %get-tuple-element.86) | copy-start | bytes 2308
  77.5 6.8 %copy-start.33 = (f32[192,1]{0,1:T(1,128)}, f32[192,1]{0,1:T(1,128)S(1)}, u32[]{:S(2)}) copy-start(f32[192,1]{0,1:T(1,128)S(1)} %get-tuple-element.87) | copy-start | bytes 2308
  77.5 6.8 %copy-start.34 = (f32[192,1]{0,1:T(1,128)}, f32[192,1]{0,1:T(1,128)S(1)}, u32[]{:S(2)}) copy-start(f32[192,1]{0,1:T(1,128)S(1)} %get-tuple-element.88) | copy-start | bytes 2308
  77.5 6.8 %copy-start.35 = (f32[192,1]{0,1:T(1,128)}, f32[192,1]{0,1:T(1,128)S(1)}, u32[]{:S(2)}) copy-start(f32[192,1]{0,1:T(1,128)S(1)} %get-tuple-element.89) | copy-start | bytes 2308
  77.5 6.8 %copy-start.36 = (f32[192,1]{0,1:T(1,128)}, f32[192,1]{0,1:T(1,128)S(1)}, u32[]{:S(2)}) copy-start(f32[192,1]{0,1:T(1,128)S(1)} %get-tuple-element.90) | copy-start | bytes 2308
  77.5 6.8 %copy-start.37 = (f32[192,1]{0,1:T(1,128)}, f32[192,1]{0,1:T(1,128)S(1)}, u32[]{:S(2)}) copy-start(f32[192,1]{0,1:T(1,128)S(1)} %get-tuple-element.91) | copy-start | bytes 2308
  77.6 6.8 %copy-start.38 = (f32[192,1]{0,1:T(1,128)}, f32[192,1]{0,1:T(1,128)S(1)}, u32[]{:S(2)}) copy-start(f32[192,1]{0,1:T(1,128)S(1)} %get-tuple-element.92) | copy-start | bytes 2308
  77.6 6.8 %copy-start.39 = (f32[192,1]{0,1:T(1,128)}, f32[192,1]{0,1:T(1,128)S(1)}, u32[]{:S(2)}) copy-start(f32[192,1]{0,1:T(1,128)S(1)} %get-tuple-element.93) | copy-start | bytes 2308
  77.6 6.8 %copy-start.40 = (f32[192,1]{0,1:T(1,128)}, f32[192,1]{0,1:T(1,128)S(1)}, u32[]{:S(2)}) copy-start(f32[192,1]{0,1:T(1,128)S(1)} %get-tuple-element.94) | copy-start | bytes 2308
  77.6 6.8 %copy-start.41 = (f32[192,1]{0,1:T(1,128)}, f32[192,1]{0,1:T(1,128)S(1)}, u32[]{:S(2)}) copy-start(f32[192,1]{0,1:T(1,128)S(1)} %get-tuple-element.95) | copy-start | bytes 2308
  77.6 6.8 %copy-start.42 = (f32[192,1]{0,1:T(1,128)}, f32[192,1]{0,1:T(1,128)S(1)}, u32[]{:S(2)}) copy-start(f32[192,1]{0,1:T(1,128)S(1)} %get-tuple-element.96) | copy-start | bytes 2308
  77.6 6.8 %copy-start.43 = (f32[192,1]{0,1:T(1,128)}, f32[192,1]{0,1:T(1,128)S(1)}, u32[]{:S(2)}) copy-start(f32[192,1]{0,1:T(1,128)S(1)} %get-tuple-element.97) | copy-start | bytes 2308
  77.6 6.8 %copy-start.44 = (f32[192,1]{0,1:T(1,128)}, f32[192,1]{0,1:T(1,128)S(1)}, u32[]{:S(2)}) copy-start(f32[192,1]{0,1:T(1,128)S(1)} %get-tuple-element.98) | copy-start | bytes 2308
  79.6 39.4 %copy-start.46 = (f32[192]{0:T(256)S(1)}, f32[192]{0:T(256)}, u32[]{:S(2)}) copy-start(f32[192]{0:T(256)} %param.13) | copy-start | bytes 2308
  141.0 15.7 %collective-permute-start.2 = (bf16[192,16]{1,0:T(8,128)(2,1)S(1)}, bf16[192,16]{1,0:T(8,128)(2,1)S(1)}, u32[]{:S(2)}, u32[]{:S(2)}) collective-permute-start(bf16[192,16]{1,0:T(8,128)(2,1)S(1)} %get-tuple-element.63), channel_id=1, source_target_pairs={{0,8},{8,16},{16,24},{24,32},{32,40},{40,48},{48,56},{56,64},{64,7... | collective-permute-start | bytes 18440 | tf_op jit(solution)/shard_map/ppermute | solution.py:27
  142.9 13.8 %collective-permute-start.3 = (bf16[192,16]{1,0:T(8,128)(2,1)S(1)}, bf16[192,16]{1,0:T(8,128)(2,1)S(1)}, u32[]{:S(2)}, u32[]{:S(2)}) collective-permute-start(bf16[192,16]{1,0:T(8,128)(2,1)S(1)} %get-tuple-element.64), channel_id=1, source_target_pairs={{8,0},{16,8},{24,16},{32,24},{40,32},{48,40},{56,48},{64,56},{72,6... | collective-permute-start | bytes 18440 | tf_op jit(solution)/shard_map/ppermute | solution.py:29
  152.0 4.9 copy-start.4
  152.0 23.7 %all-to-all-start.1 = ((bf16[8,192,512]{2,1,0:T(8,128)(2,1)}), bf16[8,192,512]{2,1,0:T(8,128)(2,1)}, u32[]{:S(2)}, u32[]{:S(2)}) async-start(bf16[8,192,512]{2,1,0:T(8,128)(2,1)} %stack.122), calls=%async_computation.1 | async-start | bytes 3145728 | tf_op jit(solution)/shard_map/all_to_all | solution.py:12
  156.5 55.9 %reduce-scatter.5.cloned.1.call-start = ((), (), s32[]{:S(2)}) async-start(), calls=%async_computation.5 | async-start | bytes 1769472 | tf_op jit(solution)/shard_map/reduce_scatter | solution.py:69
  175.7 3.2 copy-start.1
  178.9 33.5 %copy-start.14 = (f32[192]{0:T(256)S(1)}, f32[192]{0:T(256)}, u32[]{:S(2)}) copy-start(f32[192]{0:T(256)} %param.9) | copy-start | bytes 2308
  178.9 53.8 %copy-start.2 = (f32[192,1536]{1,0:T(8,128)S(1)}, f32[192,1536]{1,0:T(8,128)}, u32[]{:S(2)}) copy-start(f32[192,1536]{1,0:T(8,128)} %convolution_multiply_fusion.2) | copy-start | bytes 3538948
  232.7 321.9 %copy-start.10 = (bf16[192,512]{1,0:T(8,128)(2,1)S(1)}, bf16[192,512]{1,0:T(8,128)(2,1)}, u32[]{:S(2)}) copy-start(bf16[192,512]{1,0:T(8,128)(2,1)} %reduce-scatter.5.cloned.1.call-done) | copy-start | bytes 589828
  (7 other events, 12.7 us)
Sparse Core Ops, SparseCore 0:
  53.9 54.9 reduce-scatter.2
  166.3 46.0 reduce-scatter.4
